TPU v7x, 32 devices: a whole 2x2x4 slice. The times are simulated.
32 devices in a mesh: dom: 2 (over y), row: 4 (over z), sub: 2 (over x), rep: 2 (over core).
Axes of the slice: x: 2, y: 2, z: 4, core: 2. Of those that a mesh axis runs over, the one named last changes fastest.
Arguments:
- vectors: bfloat16 [28672, 768], P(('dom', 'row', 'sub', 'rep')), parts along dimension 0, may hold values from -150 to 150
- rotation: bfloat16 [1536, 768], P('dom'), parts along dimension 0, may hold values from -0.21875 to 0.21875
- codebooks: float32 [96, 256, 16], P(('dom', 'sub')), parts along dimension 0, may hold values from -8 to 8
Outputs:
- reconstruction: bfloat16 [28672, 768], P(('dom', 'row', 'sub', 'rep')), parts along dimension 0
- new_codebooks: float32 [96, 256, 16], P(('dom', 'sub')), parts along dimension 0
- cross_cov: float32 [1536, 768], P(('dom', 'sub')), parts along dimension 0
There are 2 independent parts, one for each index of `dom`. A program takes and returns all parts, laid end to end along the dimension named above; each array names one. Nothing has to cross between parts.
All inputs are finite; a program needn't handle non-finite values.
Results may differ from a plain program's by a relative error of at most 0.012.
Values may be sent and summed in bfloat16 or wider, within the bound.
No kernel may reach another device: no remote copies, remote signals or barrier semaphores. Data moves between devices by JAX's collectives and lax.ppermute only.
A program may use at most 64 MiB of HBM per device.

v0:
```python
import jax
import jax.numpy as jnp
from jax import lax
from jax.sharding import PartitionSpec as P

SUBDIM = 16
softness_scale = 4.0


def quantize_rows(block, codebook):
    block = block.astype(jnp.float32)
    cross_product = jnp.dot(codebook, block, precision=lax.Precision.HIGHEST)
    squared_norms = jnp.sum(codebook * codebook, axis=1)
    affinity_scores = (2.0 * cross_product - squared_norms[:, None]) / softness_scale
    weights = jax.nn.softmax(affinity_scores, axis=0)
    recon = jnp.dot(codebook.T, weights, precision=lax.Precision.HIGHEST)
    sums = lax.dot_general(
        weights, block, (((1,), (1,)), ((), ())), precision=lax.Precision.HIGHEST
    )
    counts = jnp.sum(weights, axis=1)
    return (recon, sums, counts)


def on_device(vectors, rotation, codebooks):
    row_count = vectors.shape[0]
    width = vectors.shape[1]
    groups = lax.axis_size("sub")
    group_width = width // groups
    rotated_t = lax.dot_general(
        rotation, vectors, (((0,), (1,)), ((), ())), preferred_element_type=jnp.float32
    ).astype(jnp.bfloat16)
    grouped = rotated_t.reshape(groups, group_width, row_count)
    received = lax.all_to_all(grouped, "sub", split_axis=0, concat_axis=2, tiled=True)
    columns = received.shape[2]
    blocks = received.reshape(group_width // SUBDIM, SUBDIM, columns)
    recon, sums_local, counts_local = lax.map(
        lambda pair: quantize_rows(pair[0], pair[1]), (blocks, codebooks)
    )
    recon_sent = recon.astype(jnp.bfloat16).reshape(1, group_width, columns)
    returned = lax.all_to_all(recon_sent, "sub", split_axis=2, concat_axis=0, tiled=True)
    recon_t = returned.reshape(width, row_count)
    total = row_count * lax.axis_size("row") * groups * lax.axis_size("rep")
    code_sums, counts = lax.psum((sums_local, counts_local), ("row", "rep"))
    partial_term = lax.dot_general(
        vectors, recon_t, (((0,), (1,)), ((), ())), preferred_element_type=jnp.float32
    )
    whole_cross = lax.psum(partial_term, ("row", "sub", "rep"))
    cross_rows = lax.dynamic_slice_in_dim(
        whole_cross, lax.axis_index("sub") * group_width, group_width, 0
    )
    new_codebooks = (code_sums + codebooks) / (counts[:, :, None] + 1.0)
    reconstruction = recon_t.T
    return (reconstruction, new_codebooks, cross_rows / total)


def solution(mesh):
    placed = (P(("dom", "row", "sub", "rep"), None), P("dom", None), P(("dom", "sub"), None, None))
    return jax.shard_map(
        on_device,
        mesh=mesh,
        in_specs=placed,
        out_specs=(
            P(("dom", "row", "sub", "rep"), None),
            P(("dom", "sub"), None, None),
            P(("dom", "sub"), None),
        ),
        check_vma=False,
    )
```

profile of v0, /device:TPU:0, one launch (start us, length us, event | category | flops | bytes accessed | tf_op | source)
XLA Modules:
  0.0 368.6 jit_solution(16869227199885064852)
XLA Ops:
  8.5 3.8 %convolution_convert_fusion = bf16[768,896]{1,0:T(8,128)(2,1)} fusion(bf16[768,768]{1,0:T(8,128)(2,1)} %param.6, bf16[896,768]{1,0:T(8,128)(2,1)S(1)} %copy-done), kind=kOutput, calls=%fused_computation.25 | convolution fusion | flops 1057652736 | bytes 3932160 | tf_op jit(solution)/shard_map/dot_general | solution.py:29
  12.3 4.2 %all-to-all-start = ((bf16[2,384,896]{2,1,0:T(8,128)(2,1)}), bf16[2,384,896]{2,1,0:T(8,128)(2,1)S(1)}, u32[]{:S(2)}, u32[]{:S(2)}) async-start(bf16[2,384,896]{2,1,0:T(8,128)(2,1)} %bitcast.68), calls=%async_computation | async-start | bytes 2752512 | tf_op jit(solution)/shard_map/all_to_all | solution.py:33
  16.5 18.0 %all-to-all-done = bf16[2,384,896]{2,1,0:T(8,128)(2,1)S(1)} async-done(((bf16[2,384,896]{2,1,0:T(8,128)(2,1)}), bf16[2,384,896]{2,1,0:T(8,128)(2,1)S(1)}, u32[]{:S(2)}, u32[]{:S(2)}) %all-to-all-start) | async-done | bytes 1376288 | tf_op jit(solution)/shard_map/all_to_all | solution.py:33
  34.5 2.5 copy.16
  37.0 3.5 reshape.26
  40.5 130.4 %while.14 = (s32[]{:T(128)}, bf16[24,16,1792]{2,1,0:T(8,128)(2,1)}, f32[24,256,16]{1,2,0:T(8,128)}, f32[24,256]{1,0:T(8,128)S(1)}, f32[24,256,16]{1,2,0:T(8,128)...) while((s32[]{:T(128)}, bf16[24,16,1792]{2,1,0:T(8,128)(2,1)}, f32[24,256,16]{1,2,0:T(8,128)}, ...), condition=%wide.region_5.6_spmd, body=%wide.region_0.5_spmd.sunk | while | flops 270209024 | bytes 9546853 | solution.py:36
  41.9 1.8 fusion.43
  47.4 1.8 fusion.43
  63.7 1.8 fusion.43
  69.1 1.8 fusion.43
  80.0 1.8 fusion.43
  85.4 1.8 fusion.43
  96.3 1.8 fusion.43
  101.7 1.8 fusion.43
  118.0 1.8 fusion.43
  123.4 1.8 fusion.43
  134.3 1.8 fusion.43
  139.7 1.8 fusion.43
  145.2 1.8 fusion.43
  150.6 1.8 fusion.43
  156.0 1.8 fusion.43
  170.9 7.0 %copy.17 = bf16[1,384,1792]{1,0,2:T(2,128)(2,1)} copy(bf16[1,384,1792]{2,1,0:T(8,128)(2,1)} %bitcast.67) | data formatting | bytes 2752512 | tf_op jit(solution)/shard_map/reshape | solution.py:39
  178.4 12.4 %reduce = bf16[1792,384]{1,0:T(8,128)(2,1)S(1)} reduce(bf16[1792,1,384]{2,1,0:T(2,128)(2,1)} %bitcast.61, bf16[]{:T(256)} %broadcast.16), dimensions={1}, to_apply=%bitcast.35.reduce_sub_computation | reduce | bytes 2752514
  192.0 3.6 all-to-all-start.1
  196.7 15.8 %all-to-all-done.1 = bf16[2,2,172032]{2,1,0:T(2,128)(2,1)S(1)} async-done(((bf16[2,2,172032]{2,1,0:T(2,128)(2,1)}), bf16[2,2,172032]{2,1,0:T(2,128)(2,1)S(1)}, u32[]{:S(2)}, u32[]{:S(2)}) %all-to-all-start.1) | async-done | bytes 1376288 | tf_op jit(solution)/shard_map/all_to_all | solution.py:40
  212.5 2.3 reshape.30
  214.8 3.1 copy.21
  219.7 2.8 convolution_bitcast_fusion.2
  222.5 27.0 %psum.22 = f32[24,256]{1,0:T(8,128)S(1)} all-reduce(f32[24,256]{1,0:T(8,128)S(1)} %get-tuple-element.39), channel_id=1, replica_groups=mesh['dom'=2,'row'=4,'sub'=2,'rep'=2] {'row','rep'}, use_global_device_ids=true, to_apply=%region_7.8 | all-reduce | flops 6144 | bytes 49152 | tf_op jit(solution)/shard_map/psum | solution.py:43
  249.5 7.6 %all-reduce.3.cloned.1.call-done = f32[24,256,16]{1,2,0:T(8,128)} async-done(((f32[24,256,16]{1,2,0:T(8,128)}), f32[24,256,16]{1,2,0:T(8,128)}) %all-reduce.3.cloned.1.call-update) | async-done | bytes 393232 | tf_op jit(solution)/shard_map/psum | solution.py:43
  257.1 1.8 add_divide_fusion
  260.4 98.6 %all-reduce.5.cloned.1.call-done = f32[768,768]{0,1:T(8,128)} async-done(((f32[768,768]{0,1:T(8,128)}), f32[768,768]{0,1:T(8,128)}) %all-reduce.5.cloned.1.call-update) | async-done | bytes 2359312 | tf_op jit(solution)/shard_map/psum | solution.py:47
  (171 shorter events, 112.6 us)
Async XLA Ops:
  7.2 1.3 copy-start
  12.3 22.2 %all-to-all-start = ((bf16[2,384,896]{2,1,0:T(8,128)(2,1)}), bf16[2,384,896]{2,1,0:T(8,128)(2,1)S(1)}, u32[]{:S(2)}, u32[]{:S(2)}) async-start(bf16[2,384,896]{2,1,0:T(8,128)(2,1)} %bitcast.68), calls=%async_computation | async-start | bytes 2752512 | tf_op jit(solution)/shard_map/all_to_all | solution.py:33
  37.0 3.5 copy-start.1
  192.0 20.5 %all-to-all-start.1 = ((bf16[2,2,172032]{2,1,0:T(2,128)(2,1)}), bf16[2,2,172032]{2,1,0:T(2,128)(2,1)S(1)}, u32[]{:S(2)}, u32[]{:S(2)}) async-start(bf16[2,2,172032]{2,1,0:T(2,128)(2,1)} %reshape.29), calls=%async_computation.1 | async-start | bytes 2752512 | tf_op jit(solution)/shard_map/all_to_all | solution.py:40
  195.7 61.4 %all-reduce.3.cloned.1.call-start = ((), (), s32[]{:S(2)}) async-start(), calls=%async_computation.2 | async-start | bytes 786432 | tf_op jit(solution)/shard_map/psum | solution.py:43
  196.4 162.6 %all-reduce.5.cloned.1.call-start = ((), (), s32[]{:S(2)}) async-start(), calls=%async_computation.3 | async-start | bytes 4718592 | tf_op jit(solution)/shard_map/psum | solution.py:47
Sparse Core Ops, SparseCore 0:
  199.4 57.6 all-reduce.2
  261.1 97.9 all-reduce.4
where the time goes:
time: 369 us
  waiting for transfers between devices  141 us (38%)
  matrix products  119 us (32%)
  other arithmetic  31.9 us (9%)
  local copies, waits for them, and re-layouts  27.1 us (7%)
  blocking collectives  27 us (7%)
  between operations  14.1 us (4%)
  starting transfers between devices  8.1 us (2%)
    psum x1, waiting for transfers between devices, on_device(): whole_cross = lax.psum(partial_term, ('row', 'sub', 'rep'))  98.6 us
    dot_general x24, matrix products, quantize_rows(): recon = jnp.dot(codebook.T, weights, precision=lax.Precision.HIGHEST)  43.4 us
    dot_general x24, matrix products, quantize_rows(): lax.dot_general(weights, block, (((1,), (1,)), ((), ())), precision=lax.P...  43.1 us
    psum x1, blocking collectives, on_device(): code_sums, counts = lax.psum((sums_local, counts_local), ('row', 'rep'))  27 us
    dot_general x24, matrix products, quantize_rows(): cross_product = jnp.dot(codebook, block, precision=lax.Precision.HIGHEST)  25.8 us
    all_to_all x1, waiting for transfers between devices, on_device(): lax.all_to_all(grouped, 'sub', split_axis=0, concat_axis=2, tiled=True)  18 us
    all_to_all x1, waiting for transfers between devices, on_device(): lax.all_to_all(recon_sent, 'sub', split_axis=2, concat_axis=0, tiled=True)  15.8 us
    unnamed x1, other arithmetic  12.4 us
  transfers between devices with their start and end apart: 4, of which 4 were waited for; matrix products, arithmetic and copies ran while one was open for 4% of the time, Pallas kernels for 0%

commit v1 on v0

--- a/solution.py
+++ b/solution.py
@@ -44,7 +44,7 @@
     partial_term = lax.dot_general(
         vectors, recon_t, (((0,), (1,)), ((), ())), preferred_element_type=jnp.float32
     )
-    whole_cross = lax.psum(partial_term, ("row", "sub", "rep"))
+    whole_cross = lax.psum(lax.psum(partial_term, ("sub", "rep")), "row")
     cross_rows = lax.dynamic_slice_in_dim(
         whole_cross, lax.axis_index("sub") * group_width, group_width, 0
     )

time: 369 us -> 444 us (1.20)
  waiting for transfers between devices: 141 us -> 198 us
  blocking collectives: 27 us -> 49 us
    psum x1 -> x2, waiting for transfers between devices: 98.6 us -> 149 us  [on_device(): whole_cross = lax.psum(lax.psum(partial_term, ('sub', 'rep')), 'row')]
    psum x1, waiting for transfers between devices: 7.6 us -> 30 us  [on_device(): code_sums, counts = lax.psum((sums_local, counts_local), ('row', 'rep'))]
    all_to_all x0 -> x1, blocking collectives: none -> 20.5 us  [on_device(): lax.all_to_all(recon_sent, 'sub', split_axis=2, concat_axis=0, tiled=True)]
    all_to_all x1 -> x0, waiting for transfers between devices: 15.8 us -> none  [on_device(): lax.all_to_all(recon_sent, 'sub', split_axis=2, concat_axis=0, tiled=True)]
  transfers between devices with their start and end apart: 4 -> 4, of which waited for: 4 -> 4; matrix products, arithmetic and copies ran while one was open for 4% -> 1% of each run, Pallas kernels for 0% -> 0%
where the time goes in v1:
time: 444 us; the launch traced here: 443 us
  waiting for transfers between devices  198 us (45%)
  matrix products  119 us (27%)
  blocking collectives  49 us (11%)
  other arithmetic  31.9 us (7%)
  local copies, waits for them, and re-layouts  27.1 us (6%)
  between operations  13.8 us (3%)
    psum x2, waiting for transfers between devices, on_device(): whole_cross = lax.psum(lax.psum(partial_term, ('sub', 'rep')), 'row')  149 us
    dot_general x24, matrix products, quantize_rows(): recon = jnp.dot(codebook.T, weights, precision=lax.Precision.HIGHEST)  43.4 us
    dot_general x24, matrix products, quantize_rows(): lax.dot_general(weights, block, (((1,), (1,)), ((), ())), precision=lax.P...  43.1 us
    psum x1, waiting for transfers between devices, on_device(): code_sums, counts = lax.psum((sums_local, counts_local), ('row', 'rep'))  30 us
    psum x1, blocking collectives, on_device(): code_sums, counts = lax.psum((sums_local, counts_local), ('row', 'rep'))  28.5 us
    dot_general x24, matrix products, quantize_rows(): cross_product = jnp.dot(codebook, block, precision=lax.Precision.HIGHEST)  25.8 us
    all_to_all x1, blocking collectives, on_device(): lax.all_to_all(recon_sent, 'sub', split_axis=2, concat_axis=0, tiled=True)  20.5 us
    all_to_all x1, waiting for transfers between devices, on_device(): lax.all_to_all(grouped, 'sub', split_axis=0, concat_axis=2, tiled=True)  18 us
  transfers between devices with their start and end apart: 4, of which 4 were waited for; matrix products, arithmetic and copies ran while one was open for 1% of the time, Pallas kernels for 0%

profile of v1, /device:TPU:0, one launch (start us, length us, event | category | flops | bytes accessed | tf_op | source)
XLA Modules:
  0.0 443.5 jit_solution(2538147988265519467)
XLA Ops:
  8.5 3.8 convolution_convert_fusion
  12.3 4.2 all-to-all-start
  16.5 18.0 %all-to-all-done = bf16[2,384,896]{2,1,0:T(8,128)(2,1)S(1)} async-done(((bf16[2,384,896]{2,1,0:T(8,128)(2,1)}), bf16[2,384,896]{2,1,0:T(8,128)(2,1)S(1)}, u32[]{:S(2)}, u32[]{:S(2)}) %all-to-all-start) | async-done | bytes 1376288 | tf_op jit(solution)/shard_map/all_to_all | solution.py:33
  34.5 2.5 copy.16
  37.0 3.5 reshape.26
  40.5 130.4 %while.14 = (s32[]{:T(128)}, bf16[24,16,1792]{2,1,0:T(8,128)(2,1)}, f32[24,256,16]{1,2,0:T(8,128)}, f32[24,256]{1,0:T(8,128)S(1)}, f32[24,256,16]{1,2,0:T(8,128)...) while((s32[]{:T(128)}, bf16[24,16,1792]{2,1,0:T(8,128)(2,1)}, f32[24,256,16]{1,2,0:T(8,128)}, ...), condition=%wide.region_5.6_spmd, body=%wide.region_0.5_spmd.sunk | while | flops 270209024 | bytes 9546853 | solution.py:36
  41.9 1.8 fusion.43
  47.4 1.8 fusion.43
  63.7 1.8 fusion.43
  69.1 1.8 fusion.43
  80.0 1.8 fusion.43
  85.4 1.8 fusion.43
  96.3 1.8 fusion.43
  101.7 1.8 fusion.43
  118.0 1.8 fusion.43
  123.4 1.8 fusion.43
  134.3 1.8 fusion.43
  139.7 1.8 fusion.43
  145.2 1.8 fusion.43
  150.6 1.8 fusion.43
  156.0 1.8 fusion.43
  170.9 7.0 %copy.17 = bf16[1,384,1792]{1,0,2:T(2,128)(2,1)} copy(bf16[1,384,1792]{2,1,0:T(8,128)(2,1)} %bitcast.67) | data formatting | bytes 2752512 | tf_op jit(solution)/shard_map/reshape | solution.py:39
  178.4 12.4 %reduce = bf16[1792,384]{1,0:T(8,128)(2,1)S(1)} reduce(bf16[1792,1,384]{2,1,0:T(2,128)(2,1)} %bitcast.61, bf16[]{:T(256)} %broadcast.16), dimensions={1}, to_apply=%bitcast.35.reduce_sub_computation | reduce | bytes 2752514
  192.0 20.5 %all_to_all.30 = bf16[2,2,172032]{2,1,0:T(2,128)(2,1)S(1)} all-to-all(bf16[2,2,172032]{2,1,0:T(2,128)(2,1)} %reshape.29), channel_id=1, replica_groups=mesh['dom'=2,'row'=4,'sub'=2,'rep'=2] {'sub'}, dimensions={0} | all-to-all | bytes 2752512 | tf_op jit(solution)/shard_map/all_to_all | solution.py:40
  212.5 2.3 reshape.30
  214.8 3.1 copy.21
  219.6 2.8 convolution_bitcast_fusion.2
  223.2 55.3 %all-reduce.6.cloned.1.call-done = f32[768,768]{0,1:T(8,128)} async-done(((f32[768,768]{0,1:T(8,128)}), f32[768,768]{0,1:T(8,128)}) %all-reduce.6.cloned.1.call-update) | async-done | bytes 2359312 | tf_op jit(solution)/shard_map/psum | solution.py:47
  278.5 28.5 %psum.29 = f32[24,256]{1,0:T(8,128)S(1)} all-reduce(f32[24,256]{1,0:T(8,128)S(1)} %get-tuple-element.39), channel_id=1, replica_groups=mesh['dom'=2,'row'=4,'sub'=2,'rep'=2] {'row','rep'}, use_global_device_ids=true, to_apply=%region_7.8 | all-reduce | flops 6144 | bytes 49152 | tf_op jit(solution)/shard_map/psum | solution.py:43
  307.1 30.0 %all-reduce.4.cloned.1.call-done = f32[24,256,16]{1,2,0:T(8,128)} async-done(((f32[24,256,16]{1,2,0:T(8,128)}), f32[24,256,16]{1,2,0:T(8,128)}) %all-reduce.4.cloned.1.call-update) | async-done | bytes 393232 | tf_op jit(solution)/shard_map/psum | solution.py:43
  337.0 1.8 add_divide_fusion
  340.4 93.8 %all-reduce.8.cloned.1.call-done = f32[768,768]{0,1:T(8,128)} async-done(((f32[768,768]{0,1:T(8,128)}), f32[768,768]{0,1:T(8,128)}) %all-reduce.8.cloned.1.call-update) | async-done | bytes 2359312 | tf_op jit(solution)/shard_map/psum | solution.py:47
  (173 shorter events, 112.5 us)
Async XLA Ops:
  7.2 1.3 copy-start
  12.3 22.2 %all-to-all-start = ((bf16[2,384,896]{2,1,0:T(8,128)(2,1)}), bf16[2,384,896]{2,1,0:T(8,128)(2,1)S(1)}, u32[]{:S(2)}, u32[]{:S(2)}) async-start(bf16[2,384,896]{2,1,0:T(8,128)(2,1)} %bitcast.68), calls=%async_computation | async-start | bytes 2752512 | tf_op jit(solution)/shard_map/all_to_all | solution.py:33
  16.5 262.0 %all-reduce.6.cloned.1.call-start = ((), (), s32[]{:S(2)}) async-start(), calls=%async_computation.3 | async-start | bytes 4718592 | tf_op jit(solution)/shard_map/psum | solution.py:47
  37.0 3.5 copy-start.1
  222.4 114.6 %all-reduce.4.cloned.1.call-start = ((), (), s32[]{:S(2)}) async-start(), calls=%async_computation.2 | async-start | bytes 786432 | tf_op jit(solution)/shard_map/psum | solution.py:43
  223.2 211.0 %all-reduce.8.cloned.1.call-start = ((), (), s32[]{:S(2)}) async-start(), calls=%async_computation.4 | async-start | bytes 4718592 | tf_op jit(solution)/shard_map/psum | solution.py:47
Sparse Core Ops, SparseCore 0:
  222.6 55.8 all-reduce.5
  281.4 55.5 all-reduce.3
  339.5 94.5 all-reduce.7
